TPU v7x, 32 devices: a whole 2x2x4 slice. The times are simulated.
32 devices in a mesh: px: 8 (over y, x, core), py: 4 (over z).
Axes of the slice: x: 2, y: 2, z: 4, core: 2. Of those that a mesh axis runs over, the one named last changes fastest.
Arguments:
- trial_block: float32 [8, 4, 2, 8, 8192], P('px', 'py'), may hold values from -12 to 12
- stiff_coef: float32 [8, 4, 1024], P('px', 'py'), may hold values from 0.3 to 3
- mass_coef: float32 [8, 4, 1024], P('px', 'py'), may hold values from 1 to 12
- elem_count: int32 [8, 4], P('px', 'py'), may hold values from 256 to 1024, as said below
- elem_dofs: int32 [8, 4, 1024, 20], P('px', 'py'), may hold values from 0 to 12287, as said below
- pairing: int32 [2048], replicated, may hold values from 0 to 2047, each once
- bloch_fraction: int32 [2], replicated, may hold values from 1 to 16, as said below
- stiff_ref: float32 [20, 20], replicated, may hold values from -16 to 17, as said below
- mass_ref: float32 [20, 20], replicated, may hold values from -16 to 17, as said below
Outputs:
- curl_image: float32 [8, 4, 2, 8, 8192], P('px', 'py')
- mass_image: float32 [8, 4, 2, 8, 8192], P('px', 'py')
- gram: float32 [2, 2, 8, 8], replicated
Inputs may be any that keep to these rules, and one draw needn't show every extreme that they name: `elem_count`: element slots below 128 are the only ones that name indices of 8192 or more; each part's count is at least 256, and each part of a 2-by-2 block of parts has exactly 1024 in every draw. `elem_dofs`: indices into the extended layout; slots at or above 128 name only indices below 8192. bloch_fraction[1] is 16 and 0 < bloch_fraction[0] < bloch_fraction[1]. `stiff_ref`: symmetric positive definite. `mass_ref`: symmetric positive definite.
All inputs are finite; a program needn't handle non-finite values.
Results may differ from a plain program's by a relative error of at most 0.0003.
Values sent between devices are 32-bit elements; how exact they have to be, the bound alone decides.
No kernel may reach another device: no remote copies, remote signals or barrier semaphores. Data moves between devices by JAX's collectives and lax.ppermute only.
A program may use at most 64 MiB of HBM per device.

v0:
```python
import functools
import math

import jax
import jax.numpy as jnp
from jax import lax
from jax.experimental import pallas as pl
from jax.experimental.pallas import tpu as pltpu
from jax.sharding import PartitionSpec as P

LANES = 128


def ring_route(axis, steps):
    count = lax.axis_size(axis)
    return [(source, (source + steps) % count) for source in range(count)]


def line_route(axis, distance):
    devices = range(lax.axis_size(axis))
    return [(i - distance, i) for i in devices if i - distance in devices]


def gather_lanes(table_ref, index):
    high = index // LANES
    low = index % LANES
    found = jnp.zeros_like(index)
    for r in range(table_ref.shape[0]):
        line = jnp.broadcast_to(table_ref[r : r + 1, :], index.shape)
        found = jnp.where(high == r, jnp.take_along_axis(line, low, axis=1), found)
    return found


def remap_kernel(owned_len, face_len, flag_ref, dofs_ref, pair_ref, out_ref):
    out_ref[...] = dofs_ref[...]

    @pl.when(flag_ref[0] == 1)
    def _():
        index = dofs_ref[:, :LANES]
        local = index - owned_len
        on_face = (local >= 0) & (local < face_len)
        paired = gather_lanes(pair_ref, jnp.where(on_face, local, 0))
        out_ref[:, :LANES] = jnp.where(on_face, paired + owned_len, index)


def element_kernel(
    dims,
    dofs_ref,
    count_ref,
    turn_ref,
    own_ref,
    high_x_ref,
    high_y_ref,
    pair_coef_ref,
    scale_ref,
    curl_ref,
    mass_ref,
    side_x_ref,
    side_y_ref,
    gram_ref,
    rows_x,
    gath,
    term,
    *accs,
):
    vecs, owned_len, face_len, capacity, nloc, block_rows = dims
    width = 2 * vecs
    groups = LANES // (2 * width)
    copies = LANES // width
    interior = owned_len - 2 * face_len
    extent = owned_len + 2 * face_len
    cos, sin = turn_ref[0], turn_ref[1]
    block_elems = groups * block_rows

    def turn_in(pair):
        return jnp.concatenate(
            [
                cos * pair[:vecs] - sin * pair[vecs:],
                sin * pair[:vecs] + cos * pair[vecs:],
            ],
            axis=0,
        )

    def turn_back(pair):
        return jnp.concatenate(
            [
                cos * pair[:vecs] + sin * pair[vecs:],
                cos * pair[vecs:] - sin * pair[:vecs],
            ],
            axis=0,
        )

    def put_rows(tile, first):
        rows_x[pl.ds(first, LANES), :] = jnp.concatenate([tile] * copies, axis=0).T

    zero_tile = jnp.zeros((LANES, LANES), jnp.float32)

    def build_own(c, carry):
        first = pl.multiple_of(c * LANES, LANES)
        put_rows(own_ref[:, pl.ds(first, LANES)], first)
        for acc in accs:
            acc[pl.ds(first, LANES), :] = zero_tile
        return carry

    lax.fori_loop(0, owned_len // LANES, build_own, 0)

    def build_face(c, carry):
        first = pl.multiple_of(c * LANES, LANES)
        at_x = pl.multiple_of(owned_len + first, LANES)
        at_y = pl.multiple_of(owned_len + face_len + first, LANES)
        put_rows(turn_in(high_x_ref[:, pl.ds(first, LANES)]), at_x)
        put_rows(high_y_ref[:, pl.ds(first, LANES)], at_y)
        for acc in accs:
            acc[pl.ds(at_x, LANES), :] = zero_tile
            acc[pl.ds(at_y, LANES), :] = zero_tile
        return carry

    lax.fori_loop(0, face_len // LANES, build_face, 0)

    lane = lax.broadcasted_iota(jnp.int32, (1, LANES), 1) // (2 * width)
    masks = [lane == k for k in range(groups)]

    def pick(parts):
        out = parts[-1]
        for k in range(groups - 2, -1, -1):
            out = jnp.where(masks[k], parts[k], out)
        return out

    def block(b, carry):
        first_elem = b * block_elems

        def gather_one(g, c):
            elem = first_elem + g * groups
            for i in range(nloc):
                parts = [
                    rows_x[pl.ds(dofs_ref[i * capacity + elem + k], 1), :] for k in range(groups)
                ]
                gath[pl.ds(i * block_rows + g, 1), :] = pick(parts)
            return c

        lax.fori_loop(0, block_rows, gather_one, 0)

        scale = scale_ref[pl.ds(pl.multiple_of(b * block_rows, block_rows), block_rows), :]
        values = [gath[i * block_rows : (i + 1) * block_rows, :] for i in range(nloc)]
        for j in range(nloc):
            total = pair_coef_ref[j * nloc] * values[0]
            for i in range(1, nloc):
                total = total + pair_coef_ref[j * nloc + i] * values[i]
            term[j * block_rows : (j + 1) * block_rows, :] = total * scale

        def scatter_one(g, c):
            elem = first_elem + g * groups
            for j in range(nloc):
                row = term[pl.ds(j * block_rows + g, 1), :]
                for k in range(groups):
                    at = pl.ds(dofs_ref[j * capacity + elem + k], 1)
                    accs[k][at, :] = accs[k][at, :] + row
            return c

        lax.fori_loop(0, block_rows, scatter_one, 0)
        return carry

    live = count_ref[0]
    lax.fori_loop(0, (live + block_elems - 1) // block_elems, block, 0)

    def folded(first):
        at = pl.ds(first, LANES)
        turned = pick([acc[at, :] for acc in accs]).T
        total = turned[: 2 * width]
        for k in range(1, groups):
            total = total + turned[k * 2 * width : (k + 1) * 2 * width]
        return total

    def split(x):
        top = x.astype(jnp.bfloat16)
        return top, (x - top.astype(jnp.float32)).astype(jnp.bfloat16)

    def inner(x, y):
        def one(p, q):
            return lax.dot_general(
                p, q, (((1,), (1,)), ((), ())), preferred_element_type=jnp.float32
            )

        xt, xb = split(x)
        yt, yb = split(y)
        return one(xt, yt) + (one(xt, yb) + one(xb, yt))

    gram_ref[...] = jnp.zeros_like(gram_ref)

    def fold_own(c, carry):
        first = pl.multiple_of(c * LANES, LANES)
        at = pl.ds(first, LANES)
        total = folded(first)
        curl_ref[:, at] = total[:width]
        mass_ref[:, at] = total[width:]
        gram_ref[...] += inner(own_ref[:, at], total)
        return carry

    lax.fori_loop(0, owned_len // LANES, fold_own, 0)

    def fold_face(c, carry):
        first = pl.multiple_of(c * LANES, LANES)
        at = pl.ds(first, LANES)
        total = folded(pl.multiple_of(owned_len + first, LANES))
        gram_ref[...] += inner(turn_in(high_x_ref[:, at]), total)
        side_x_ref[:width, at] = turn_back(total[:width])
        side_x_ref[width:, at] = turn_back(total[width:])
        total = folded(pl.multiple_of(owned_len + face_len + first, LANES))
        gram_ref[...] += inner(high_y_ref[:, at], total)
        side_y_ref[:, at] = total
        return carry

    lax.fori_loop(0, face_len // LANES, fold_face, 0)


def all_sum(value, axis):
    count = lax.axis_size(axis)
    step = 1
    total = value
    while step < count:
        total = total + lax.ppermute(total, axis, [(i, i ^ step) for i in range(count)])
        step *= 2
    return total


def on_device(
    trial_block,
    stiff_coef,
    mass_coef,
    elem_count,
    elem_dofs,
    pairing,
    bloch_fraction,
    stiff_ref,
    mass_ref,
):
    own_block = trial_block[0, 0]
    vecs, owned_len = own_block.shape[1:]
    face_len = pairing.shape[0]
    interior = owned_len - 2 * face_len
    width = 2 * vecs
    groups = LANES // (2 * width)
    capacity, nloc = elem_dofs.shape[2:]
    phase_angle = (
        2.0
        * math.pi
        * bloch_fraction[0].astype(jnp.float32)
        / bloch_fraction[1].astype(jnp.float32)
    )
    at_end = lax.axis_index("px") == lax.axis_size("px") - 1
    turn = jnp.where(
        at_end,
        jnp.stack([jnp.cos(phase_angle), jnp.sin(phase_angle)]),
        jnp.array([1.0, 0.0], jnp.float32),
    )
    own_rows = own_block.reshape(width, owned_len)
    low_x = own_rows[:, interior : interior + face_len]
    low_y = own_rows[:, interior + face_len :]
    high_x = lax.ppermute(low_x, "px", ring_route("px", -1))
    high_y = lax.ppermute(low_y, "py", line_route("py", -1))

    slot_dofs = elem_dofs[0, 0].T
    remapped = pl.pallas_call(
        functools.partial(remap_kernel, owned_len, face_len),
        out_shape=jax.ShapeDtypeStruct(slot_dofs.shape, jnp.int32),
        in_specs=[
            pl.BlockSpec(memory_space=pltpu.SMEM),
            pl.BlockSpec(memory_space=pltpu.VMEM),
            pl.BlockSpec(memory_space=pltpu.VMEM),
        ],
        out_specs=pl.BlockSpec(memory_space=pltpu.VMEM),
        name="remap",
    )(at_end.astype(jnp.int32).reshape(1), slot_dofs, pairing.reshape(-1, LANES))
    flat_dofs = remapped.reshape(-1)

    coefs = jnp.stack([stiff_ref.reshape(-1), mass_ref.reshape(-1)], axis=1)
    block_rows = 8
    pair_coef = jnp.broadcast_to(
        coefs[:, None, None, :, None], (nloc * nloc, block_rows, groups, 2, width)
    ).reshape(nloc * nloc, block_rows, LANES)
    live = elem_count[0]
    slot_live = jnp.arange(capacity, dtype=jnp.int32) < live[0]
    scales = jnp.where(slot_live[None], jnp.stack([stiff_coef[0, 0], mass_coef[0, 0]]), 0.0)
    scale = jnp.broadcast_to(
        scales.reshape(2, capacity // groups, groups).transpose(1, 2, 0)[..., None],
        (capacity // groups, groups, 2, width),
    ).reshape(capacity // groups, LANES)

    extent = owned_len + 2 * face_len
    dims = (vecs, owned_len, face_len, capacity, nloc, block_rows)
    curl, mass, side_x, side_y, gram = pl.pallas_call(
        functools.partial(element_kernel, dims),
        out_shape=(
            jax.ShapeDtypeStruct((width, owned_len), jnp.float32),
            jax.ShapeDtypeStruct((width, owned_len), jnp.float32),
            jax.ShapeDtypeStruct((2 * width, face_len), jnp.float32),
            jax.ShapeDtypeStruct((2 * width, face_len), jnp.float32),
            jax.ShapeDtypeStruct((width, 2 * width), jnp.float32),
        ),
        in_specs=[pl.BlockSpec(memory_space=pltpu.SMEM)] * 3
        + [pl.BlockSpec(memory_space=pltpu.VMEM)] * 5,
        out_specs=[pl.BlockSpec(memory_space=pltpu.VMEM)] * 5,
        scratch_shapes=[
            pltpu.VMEM((extent, LANES), jnp.float32),
            pltpu.VMEM((nloc * block_rows, LANES), jnp.float32),
            pltpu.VMEM((nloc * block_rows, LANES), jnp.float32),
        ]
        + [pltpu.VMEM((extent, LANES), jnp.float32)] * groups,
        compiler_params=pltpu.CompilerParams(vmem_limit_bytes=60 * 1024 * 1024),
        name="elements",
    )(flat_dofs, live, turn, own_rows, high_x, high_y, pair_coef, scale)

    back_x = lax.ppermute(side_x, "px", ring_route("px", 1))
    back_y = lax.ppermute(side_y, "py", line_route("py", 1))

    def finish(image, part):
        add_x = back_x[part * width : (part + 1) * width]
        add_y = back_y[part * width : (part + 1) * width]
        whole = image.at[:, interior:].add(jnp.concatenate([add_x, add_y], axis=1))
        return whole.reshape(1, 1, 2, vecs, owned_len)

    summed = all_sum(all_sum(gram, "px"), "py")
    parts = summed.reshape(2, vecs, 2, 2, vecs)
    real_part = parts[0, :, :, 0] + parts[1, :, :, 1]
    imag_part = parts[0, :, :, 1] - parts[1, :, :, 0]
    divisor = float(lax.axis_size("px") * lax.axis_size("py") * owned_len)
    gram_out = jnp.stack([real_part, imag_part]).transpose(2, 0, 1, 3) / divisor
    return (finish(curl, 0), finish(mass, 1), gram_out)


def solution(mesh):
    return jax.shard_map(
        on_device,
        mesh=mesh,
        in_specs=(
            P("px", "py", None, None, None),
            P("px", "py", None),
            P("px", "py", None),
            P("px", "py"),
            P("px", "py", None, None),
            P(),
            P(),
            P(),
            P(),
        ),
        out_specs=(P("px", "py", None, None, None), P("px", "py", None, None, None), P()),
        check_vma=False,
    )
```

profile of v0, /device:TPU:0, one launch (start us, length us, event | category | flops | bytes accessed | tf_op | source)
XLA Modules:
  0.0 127.1 jit_solution(8851048339870285909)
XLA Ops:
  0.6 0.0 copy-start.2
  0.6 1.0 fusion.6
  1.6 1.3 %collective-permute-start.1 = (f32[16,2048]{1,0:T(8,128)S(1)}, f32[16,2048]{1,0:T(8,128)S(1)}, u32[]{:S(2)}, u32[]{:S(2)}) collective-permute-start(f32[16,2048]{1,0:T(8,128)S(1)} %get-tuple-element.46), channel_id=1, source_target_pairs={{1,0},{2,1},{3,2},{5,4},{6,5},{7,6},{9,8},{10,9},{11,10},{13,12},{... | collective-permute-start | bytes 393224 | tf_op jit(solution)/shard_map/ppermute | solution.py:260
  2.9 3.4 %collective-permute-start = (f32[16,2048]{1,0:T(8,128)S(1)}, f32[16,2048]{1,0:T(8,128)S(1)}, u32[]{:S(2)}, u32[]{:S(2)}) collective-permute-start(f32[16,2048]{1,0:T(8,128)S(1)} %get-tuple-element.47), channel_id=1, source_target_pairs={{0,28},{4,0},{8,4},{12,8},{16,12},{20,16},{24,20},{28,24},{1,29},{... | collective-permute-start | bytes 393224 | tf_op jit(solution)/shard_map/ppermute | solution.py:259
  6.4 1.3 %fusion.10 = (s32[1]{0:T(128)}, s32[1]{0:T(128)}) fusion(s32[2]{0:T(128)} %param.20), kind=kLoop, calls=%fused_computation.20 | loop fusion | bytes 16 | tf_op jit(solution)/shard_map/slice | solution.py:248
  9.8 0.8 stack_reshape.6
  10.6 0.8 stack_reshape.7
  11.4 0.5 broadcast.52
  11.9 1.3 %reduce.11 = f32[1024]{0:T(1024)S(1)} reduce(f32[1,1,1024]{2,1,0:T(1,128)} %param.15, f32[]{:T(128)} %broadcast.52), dimensions={0,1}, to_apply=%param.15.reduce_sub_computation.3 | reduce | bytes 8196 | tf_op args[1]
  13.3 1.3 %reduce.10 = f32[1024]{0:T(1024)S(1)} reduce(f32[1,1,1024]{2,1,0:T(1,128)} %param.16, f32[]{:T(128)} %broadcast.52), dimensions={0,1}, to_apply=%param.16.reduce_sub_computation.3 | reduce | bytes 8196 | tf_op args[2]
  14.6 1.5 %copy.52 = s32[1,1,1024,20]{2,3,1,0:T(8,128)} copy(s32[1,1,1024,20]{2,1,3,0:T(1,128)} %param.18) | data formatting | bytes 163840
  16.2 1.5 %remap.1 = s32[20,1024]{1,0:T(8,128)} custom-call(s32[1]{0:T(128)} %bitcast.flag_ref, s32[20,1024]{1,0:T(8,128)} %bitcast.28, s32[16,128]{1,0:T(8,128)} %bitcast.31), custom_call_target="tpu_custom_call" | custom-call | tf_op jit(solution)/shard_map/remap/pallas_call | solution.py:263
  17.7 1.5 %reshape.144.dofs_ref = s32[20480]{0:T(1024)} reshape(s32[20,1024]{1,0:T(8,128)} %remap.1) | data formatting | bytes 163840 | tf_op jit(solution)/shard_map/reshape | solution.py:274
  19.3 0.1 stack.23
  19.4 0.1 copy.30
  19.5 0.1 stack.22
  19.6 0.1 copy.29
  19.8 0.8 copy.32.scale_ref
  20.6 0.1 copy.28
  20.7 0.0 copy-done.2
  20.7 0.6 broadcast_select_fusion.turn_ref
  21.3 0.0 collective-permute-done.1.high_y_ref
  21.3 0.0 copy-start
  21.3 0.0 collective-permute-done.high_x_ref
  21.3 0.0 copy-start.1
  21.3 1.3 %broadcast_in_dim.31.pair_coef_ref = f32[400,8,128]{2,1,0:T(8,128)} broadcast(f32[400,128]{1,0:T(8,128)S(1)} %copy.28), dimensions={0,2} | broadcast | bytes 1843200 | tf_op jit(solution)/shard_map/broadcast_in_dim | solution.py:278
  22.6 0.0 copy-done
  22.6 0.0 copy-done.1
  22.6 47.1 %elements.1 = (f32[16,8192]{1,0:T(8,128)}, f32[16,8192]{1,0:T(8,128)}, f32[32,2048]{1,0:T(8,128)}, f32[32,2048]{1,0:T(8,128)}, f32[16,32]{1,0:T(8,128)}) custom-call(s32[20480]{0:T(1024)} %reshape.144.dofs_ref, s32[1]{0:T(128)} %bitcast.22.count_ref, f32[2]{0:T(128)} %broadcast_select_fusion.turn_ref, f32[16,8192]{1,0:T(8,128)} %bitcast.25, ...), custom_call_target="tpu_custom_call" | custom-call | tf_op jit(solution)/shard_map/elements/pallas_call | solution.py:291
  69.7 0.0 collective-permute-start.4
  69.7 1.4 %collective-permute-done.4 = f32[16,32]{1,0:T(8,128)S(1)} collective-permute-done((f32[16,32]{1,0:T(8,128)}, f32[16,32]{1,0:T(8,128)S(1)}, u32[]{:S(2)}, u32[]{:S(2)}) %collective-permute-start.4) | collective-permute-done | bytes 2080 | tf_op jit(solution)/shard_map/ppermute | solution.py:221
  71.1 0.7 add.45
  71.8 7.4 %collective-permute-start.5 = (f32[16,32]{1,0:T(8,128)S(1)}, f32[16,32]{1,0:T(8,128)S(1)}, u32[]{:S(2)}, u32[]{:S(2)}) collective-permute-start(f32[16,32]{1,0:T(8,128)S(1)} %add.45), channel_id=1, source_target_pairs={{0,8},{4,12},{8,0},{12,4},{16,24},{20,28},{24,16},{28,20},{1,9},{5... | collective-permute-start | bytes 6152 | tf_op jit(solution)/shard_map/ppermute | solution.py:221
  79.2 1.6 %collective-permute-done.5 = f32[16,32]{1,0:T(8,128)S(1)} collective-permute-done((f32[16,32]{1,0:T(8,128)S(1)}, f32[16,32]{1,0:T(8,128)S(1)}, u32[]{:S(2)}, u32[]{:S(2)}) %collective-permute-start.5) | collective-permute-done | bytes 2080 | tf_op jit(solution)/shard_map/ppermute | solution.py:221
  80.8 0.2 collective-permute-start.6
  81.0 3.5 %collective-permute-done.6 = f32[16,32]{1,0:T(8,128)S(1)} collective-permute-done((f32[16,32]{1,0:T(8,128)S(1)}, f32[16,32]{1,0:T(8,128)S(1)}, u32[]{:S(2)}, u32[]{:S(2)}) %collective-permute-start.6) | collective-permute-done | bytes 2080 | tf_op jit(solution)/shard_map/ppermute | solution.py:221
  84.5 27.2 %collective-permute-start.7 = (f32[16,32]{1,0:T(8,128)S(1)}, f32[16,32]{1,0:T(8,128)S(1)}, u32[]{:S(2)}, u32[]{:S(2)}) collective-permute-start(f32[16,32]{1,0:T(8,128)S(1)} %add.47), channel_id=1, source_target_pairs={{0,1},{1,0},{2,3},{3,2},{4,5},{5,4},{6,7},{7,6},{8,9},{9,8},{10,11... | collective-permute-start | bytes 6152 | tf_op jit(solution)/shard_map/ppermute | solution.py:221
  111.7 1.6 %collective-permute-done.7 = f32[16,32]{1,0:T(8,128)S(1)} collective-permute-done((f32[16,32]{1,0:T(8,128)S(1)}, f32[16,32]{1,0:T(8,128)S(1)}, u32[]{:S(2)}, u32[]{:S(2)}) %collective-permute-start.7) | collective-permute-done | bytes 2080 | tf_op jit(solution)/shard_map/ppermute | solution.py:221
  113.3 3.5 %collective-permute-start.8 = (f32[16,32]{1,0:T(8,128)S(1)}, f32[16,32]{1,0:T(8,128)S(1)}, u32[]{:S(2)}, u32[]{:S(2)}) collective-permute-start(f32[16,32]{1,0:T(8,128)S(1)} %add.48), channel_id=1, source_target_pairs={{0,2},{1,3},{2,0},{3,1},{4,6},{5,7},{6,4},{7,5},{8,10},{9,11},{10,... | collective-permute-start | bytes 6152 | tf_op jit(solution)/shard_map/ppermute | solution.py:221
  116.8 0.0 collective-permute-start.2
  116.8 1.9 %collective-permute-start.3 = (f32[32,2048]{1,0:T(8,128)}, f32[32,2048]{1,0:T(8,128)S(1)}, u32[]{:S(2)}, u32[]{:S(2)}) collective-permute-start(f32[32,2048]{1,0:T(8,128)} %get-tuple-element.34), channel_id=1, source_target_pairs={{0,1},{1,2},{2,3},{4,5},{5,6},{6,7},{8,9},{9,10},{10,11},{12,13},{... | collective-permute-start | bytes 786440 | tf_op jit(solution)/shard_map/ppermute | solution.py:314
  118.7 0.0 collective-permute-done.8
  118.7 0.1 reshape.148
  118.9 0.6 copy.37
  119.5 4.2 %collective-permute-done.2 = f32[32,2048]{1,0:T(8,128)S(1)} collective-permute-done((f32[32,2048]{1,0:T(8,128)}, f32[32,2048]{1,0:T(8,128)S(1)}, u32[]{:S(2)}, u32[]{:S(2)}) %collective-permute-start.2) | collective-permute-done | bytes 262176 | tf_op jit(solution)/shard_map/ppermute | solution.py:313
  123.7 1.5 %collective-permute-done.3 = f32[32,2048]{1,0:T(8,128)S(1)} collective-permute-done((f32[32,2048]{1,0:T(8,128)}, f32[32,2048]{1,0:T(8,128)S(1)}, u32[]{:S(2)}, u32[]{:S(2)}) %collective-permute-start.3) | collective-permute-done | bytes 262176 | tf_op jit(solution)/shard_map/ppermute | solution.py:314
  125.2 1.9 %fusion = (f32[16,8192]{1,0:T(8,128)}, f32[16,8192]{1,0:T(8,128)}) fusion(f32[16,8192]{1,0:T(8,128)} %get-tuple-element.32, f32[16,2048]{1,0:T(8,128)S(1)} %get-tuple-element.51, f32[16,2048]{1,0:T(8,128)S(1)} %get-tuple-element.49, f32[16,8192]{1,0:T(8,128)} %get-tuple-element.35, f32[16,2048]{1,0:T(8,128)S(1)} %get-tuple-element.50, ...), kind=kLoop, calls=%fused_computation.1 | loop fusion | flops 262144 | bytes 1572864 | tf_op jit(solution)/shard_map/scatter-add | solution.py:319
  (15 shorter events, 0.2 us)
Async XLA Ops:
  0.6 20.1 %copy-start.2 = (f32[2]{0:T(128)S(1)}, f32[2]{0:T(128)}, u32[]{:S(2)}) copy-start(f32[2]{0:T(128)} %constant.70.clone) | copy-start | bytes 28
  1.6 19.6 %collective-permute-start.1 = (f32[16,2048]{1,0:T(8,128)S(1)}, f32[16,2048]{1,0:T(8,128)S(1)}, u32[]{:S(2)}, u32[]{:S(2)}) collective-permute-start(f32[16,2048]{1,0:T(8,128)S(1)} %get-tuple-element.46), channel_id=1, source_target_pairs={{1,0},{2,1},{3,2},{5,4},{6,5},{7,6},{9,8},{10,9},{11,10},{13,12},{... | collective-permute-start | bytes 393224 | tf_op jit(solution)/shard_map/ppermute | solution.py:260
  2.9 18.4 %collective-permute-start = (f32[16,2048]{1,0:T(8,128)S(1)}, f32[16,2048]{1,0:T(8,128)S(1)}, u32[]{:S(2)}, u32[]{:S(2)}) collective-permute-start(f32[16,2048]{1,0:T(8,128)S(1)} %get-tuple-element.47), channel_id=1, source_target_pairs={{0,28},{4,0},{8,4},{12,8},{16,12},{20,16},{24,20},{28,24},{1,29},{... | collective-permute-start | bytes 393224 | tf_op jit(solution)/shard_map/ppermute | solution.py:259
  21.3 1.3 %copy-start = (f32[16,2048]{1,0:T(8,128)}, f32[16,2048]{1,0:T(8,128)S(1)}, u32[]{:S(2)}) copy-start(f32[16,2048]{1,0:T(8,128)S(1)} %collective-permute-done.1.high_y_ref) | copy-start | bytes 393220
  21.3 1.3 %copy-start.1 = (f32[16,2048]{1,0:T(8,128)}, f32[16,2048]{1,0:T(8,128)S(1)}, u32[]{:S(2)}) copy-start(f32[16,2048]{1,0:T(8,128)S(1)} %collective-permute-done.high_x_ref) | copy-start | bytes 393220
  69.7 1.4 %collective-permute-start.4 = (f32[16,32]{1,0:T(8,128)}, f32[16,32]{1,0:T(8,128)S(1)}, u32[]{:S(2)}, u32[]{:S(2)}) collective-permute-start(f32[16,32]{1,0:T(8,128)} %get-tuple-element.36), channel_id=1, source_target_pairs={{0,4},{4,0},{8,12},{12,8},{16,20},{20,16},{24,28},{28,24},{1,5},{5... | collective-permute-start | bytes 6152 | tf_op jit(solution)/shard_map/ppermute | solution.py:221
  71.8 9.0 %collective-permute-start.5 = (f32[16,32]{1,0:T(8,128)S(1)}, f32[16,32]{1,0:T(8,128)S(1)}, u32[]{:S(2)}, u32[]{:S(2)}) collective-permute-start(f32[16,32]{1,0:T(8,128)S(1)} %add.45), channel_id=1, source_target_pairs={{0,8},{4,12},{8,0},{12,4},{16,24},{20,28},{24,16},{28,20},{1,9},{5... | collective-permute-start | bytes 6152 | tf_op jit(solution)/shard_map/ppermute | solution.py:221
  80.8 3.7 %collective-permute-start.6 = (f32[16,32]{1,0:T(8,128)S(1)}, f32[16,32]{1,0:T(8,128)S(1)}, u32[]{:S(2)}, u32[]{:S(2)}) collective-permute-start(f32[16,32]{1,0:T(8,128)S(1)} %add.46), channel_id=1, source_target_pairs={{0,16},{4,20},{8,24},{12,28},{16,0},{20,4},{24,8},{28,12},{1,17},{... | collective-permute-start | bytes 6152 | tf_op jit(solution)/shard_map/ppermute | solution.py:221
  84.5 28.8 %collective-permute-start.7 = (f32[16,32]{1,0:T(8,128)S(1)}, f32[16,32]{1,0:T(8,128)S(1)}, u32[]{:S(2)}, u32[]{:S(2)}) collective-permute-start(f32[16,32]{1,0:T(8,128)S(1)} %add.47), channel_id=1, source_target_pairs={{0,1},{1,0},{2,3},{3,2},{4,5},{5,4},{6,7},{7,6},{8,9},{9,8},{10,11... | collective-permute-start | bytes 6152 | tf_op jit(solution)/shard_map/ppermute | solution.py:221
  113.3 5.4 %collective-permute-start.8 = (f32[16,32]{1,0:T(8,128)S(1)}, f32[16,32]{1,0:T(8,128)S(1)}, u32[]{:S(2)}, u32[]{:S(2)}) collective-permute-start(f32[16,32]{1,0:T(8,128)S(1)} %add.48), channel_id=1, source_target_pairs={{0,2},{1,3},{2,0},{3,1},{4,6},{5,7},{6,4},{7,5},{8,10},{9,11},{10,... | collective-permute-start | bytes 6152 | tf_op jit(solution)/shard_map/ppermute | solution.py:221
  116.8 6.9 %collective-permute-start.2 = (f32[32,2048]{1,0:T(8,128)}, f32[32,2048]{1,0:T(8,128)S(1)}, u32[]{:S(2)}, u32[]{:S(2)}) collective-permute-start(f32[32,2048]{1,0:T(8,128)} %get-tuple-element.33), channel_id=1, source_target_pairs={{0,4},{4,8},{8,12},{12,16},{16,20},{20,24},{24,28},{28,0},{1,5},{5... | collective-permute-start | bytes 786440 | tf_op jit(solution)/shard_map/ppermute | solution.py:313
  116.8 8.4 %collective-permute-start.3 = (f32[32,2048]{1,0:T(8,128)}, f32[32,2048]{1,0:T(8,128)S(1)}, u32[]{:S(2)}, u32[]{:S(2)}) collective-permute-start(f32[32,2048]{1,0:T(8,128)} %get-tuple-element.34), channel_id=1, source_target_pairs={{0,1},{1,2},{2,3},{4,5},{5,6},{6,7},{8,9},{9,10},{10,11},{12,13},{... | collective-permute-start | bytes 786440 | tf_op jit(solution)/shard_map/ppermute | solution.py:314
where the time goes:
time: 128 us; the launch traced here: 127 us
  Pallas kernels  48.6 us (38%)
  starting transfers between devices  44.9 us (35%)
  waiting for transfers between devices  13.8 us (11%)
  local copies, waits for them, and re-layouts  10.9 us (9%)
  other arithmetic  5.91 us (5%)
  between operations  2.96 us (2%)
    pallas_call x1, Pallas kernels, on_device(): pl.pallas_call(functools.partial(element_kernel, dims), out_shape=(jax.Sh...  47.1 us
    ppermute x5, starting transfers between devices, all_sum(): lax.ppermute(total, axis, [(i, i ^ step) for i in range(count)])  38.3 us
    ppermute x5, waiting for transfers between devices, all_sum(): lax.ppermute(total, axis, [(i, i ^ step) for i in range(count)])  8.1 us
    ppermute x1, waiting for transfers between devices, on_device(): back_x = lax.ppermute(side_x, 'px', ring_route('px', 1))  4.2 us
    ppermute x1, starting transfers between devices, on_device(): high_x = lax.ppermute(low_x, 'px', ring_route('px', -1))  3.41 us
    unnamed x2, other arithmetic  2.69 us
    unnamed x9, local copies, waits for them, and re-layouts  2.68 us
  transfers between devices with their start and end apart: 9, of which 6 were waited for; matrix products, arithmetic and copies ran while one was open for 9% of the time, Pallas kernels for 1%

commit v1 on v0

v1 whole, which is shorter than its diff:
```python
import functools
import math

import jax
import jax.numpy as jnp
from jax import lax
from jax.experimental import pallas as pl
from jax.experimental.pallas import tpu as pltpu
from jax.sharding import PartitionSpec as P

LANES = 128
BLOCK_ROWS = 8
F32 = jnp.float32
BF16 = jnp.bfloat16


def ring_route(axis, steps):
    count = lax.axis_size(axis)
    return [(source, (source + steps) % count) for source in range(count)]


def line_route(axis, distance):
    devices = range(lax.axis_size(axis))
    return [(i - distance, i) for i in devices if i - distance in devices]


def iota(shape, axis):
    return lax.broadcasted_iota(jnp.int32, shape, axis)


def split(x):
    top = x.astype(BF16)
    return top, (x - top.astype(F32)).astype(BF16)


def dot_nt(left, right):
    return lax.dot_general(
        left, right, (((1,), (1,)), ((), ())), preferred_element_type=F32
    )


def gather_lanes(table_ref, index):
    high = index // LANES
    low = index % LANES
    found = jnp.zeros_like(index)
    for r in range(table_ref.shape[0]):
        line = jnp.broadcast_to(table_ref[r : r + 1, :], index.shape)
        found = jnp.where(high == r, jnp.take_along_axis(line, low, axis=1), found)
    return found


def prepare_kernel(
    owned_len, face_len, width, count_ref, bloch_ref, dofs_ref, pair_ref, stiff_ref, mass_ref,
    table_ref, scale_ref, turn_ref,
):
    capacity, nloc = dofs_ref.shape
    rows = table_ref.shape[0]
    groups = LANES // (2 * width)
    at_end = lax.axis_index("px") == lax.axis_size("px") - 1
    per_chunk = LANES // groups
    lane_of = iota((LANES, LANES), 0)
    elem_of = iota((LANES, LANES), 1)
    mine = elem_of % groups == lane_of // (2 * width)
    is_curl = lane_of // width % 2 == 0
    chooser = (iota((per_chunk, LANES), 1) // groups == iota((per_chunk, LANES), 0)).astype(BF16)
    chooser = jnp.concatenate([chooser, chooser], axis=1)
    live = count_ref[0]
    for c in range(capacity // LANES):
        at = slice(c * LANES, (c + 1) * LANES)
        tile = jnp.concatenate(
            [dofs_ref[at, :], jnp.zeros((LANES, LANES - nloc), jnp.int32)], axis=1
        ).T
        index = tile[:rows]
        slot_row = iota((rows, LANES), 0)
        after = jnp.concatenate([index[1:], index[:1]], axis=0)
        clash = (index == after) & (slot_row % 2 == 0) & (slot_row + 1 < nloc)
        flag = jnp.max(clash.astype(jnp.int32), axis=0, keepdims=True)
        flag = jnp.broadcast_to(flag, (8, LANES))
        reach = groups * BLOCK_ROWS // 2
        while reach:
            flag = jnp.maximum(flag, pltpu.roll(flag, reach, 1))
            reach //= 2
        index = jnp.where(slot_row == nloc, flag[:1], index)
        table_ref[:, at] = index
        scales = jnp.where(is_curl, stiff_ref[:, at], mass_ref[:, at])
        scales = jnp.where(mine & (c * LANES + elem_of < live), scales, 0.0)
        scale_ref[c * per_chunk : (c + 1) * per_chunk, :] = dot_nt(
            chooser, jnp.concatenate(split(scales), axis=1)
        )

    @pl.when(at_end)
    def _():
        index = table_ref[:, :LANES]
        local = index - owned_len
        on_face = (local >= 0) & (local < face_len) & (iota((rows, LANES), 0) < nloc)
        paired = gather_lanes(pair_ref, jnp.where(on_face, local, 0))
        table_ref[:, :LANES] = jnp.where(on_face, paired + owned_len, index)

    ratio = jnp.full((8, LANES), bloch_ref[0].astype(F32), F32) / bloch_ref[1].astype(F32)
    angle = (2.0 * math.pi) * jnp.where(at_end, ratio, 0.0)
    turn_ref[:8] = jnp.cos(angle)
    turn_ref[8:] = jnp.sin(angle)


def element_kernel(
    width,
    count_ref,
    stiff_ref,
    mass_ref,
    table_hbm,
    turn_ref,
    own_ref,
    high_x_ref,
    high_y_ref,
    scale_ref,
    curl_ref,
    mass_out_ref,
    side_x_ref,
    side_y_ref,
    gram_ref,
    dofs_ref,
    pair_coef,
    rows_x,
    gath,
    term,
    sems,
    *accs,
):
    owned_len = own_ref.shape[1]
    face_len = high_x_ref.shape[1]
    vecs = width // 2
    nloc = stiff_ref.shape[0]
    capacity = table_hbm.shape[1]
    block_rows = BLOCK_ROWS
    groups = LANES // (2 * width)
    copies = LANES // width
    block_elems = groups * block_rows

    loads = [
        pltpu.make_async_copy(
            table_hbm.at[i], dofs_ref.at[pl.ds(i * capacity, capacity)], sems.at[i]
        )
        for i in range(nloc + 1)
    ]
    for load in loads:
        load.start()

    cos, sin = turn_ref[:vecs], turn_ref[8 : 8 + vecs]

    def turn_in(pair):
        n = pair.shape[1] // LANES
        c, s = jnp.concatenate([cos] * n, axis=1), jnp.concatenate([sin] * n, axis=1)
        a, b = pair[:vecs], pair[vecs:]
        return jnp.concatenate([c * a - s * b, s * a + c * b], axis=0)

    def turn_back(pair):
        n = pair.shape[1] // LANES
        c, s = jnp.concatenate([cos] * n, axis=1), jnp.concatenate([sin] * n, axis=1)
        a, b = pair[:vecs], pair[vecs:]
        return jnp.concatenate([c * a + s * b, c * b - s * a], axis=0)

    unit = (iota((LANES, LANES), 0) == iota((LANES, LANES), 1)).astype(BF16)
    unit = jnp.concatenate([unit, unit], axis=1)
    zero_tile = jnp.zeros((LANES, LANES), F32)

    def put_rows(tile, first):
        top, low = split(tile)
        tiled = jnp.concatenate(
            [jnp.concatenate([top] * copies, axis=0), jnp.concatenate([low] * copies, axis=0)],
            axis=1,
        )
        rows_x[pl.ds(first, LANES), :] = dot_nt(unit, tiled)
        for acc in accs:
            acc[pl.ds(first, LANES), :] = zero_tile

    span = 4 * LANES

    def build_own(c, carry):
        for u in range(span // LANES):
            first = pl.multiple_of(c * span + u * LANES, LANES)
            put_rows(own_ref[:, pl.ds(first, LANES)], first)
        return carry

    lax.fori_loop(0, owned_len // span, build_own, 0)

    def build_face(c, carry):
        for u in range(2):
            first = pl.multiple_of(c * 2 * LANES + u * LANES, LANES)
            put_rows(
                turn_in(high_x_ref[:, pl.ds(first, LANES)]),
                pl.multiple_of(owned_len + first, LANES),
            )
            put_rows(
                high_y_ref[:, pl.ds(first, LANES)],
                pl.multiple_of(owned_len + face_len + first, LANES),
            )
        return carry

    lax.fori_loop(0, face_len // (2 * LANES), build_face, 0)

    curl_lane = iota((8, LANES), 1) // width % 2 == 0

    def build_coef(j, carry):
        for i in range(nloc):
            pair_coef[j * nloc + i] = jnp.where(curl_lane, stiff_ref[j, i], mass_ref[j, i])
        return carry

    lax.fori_loop(0, nloc, build_coef, 0)

    for load in loads:
        load.wait()

    lane = iota((1, LANES), 1) // (2 * width)
    masks = [lane == k for k in range(groups)]

    def pick(parts):
        out = parts[-1]
        for k in range(groups - 2, -1, -1):
            out = jnp.where(masks[k], parts[k], out)
        return out

    def index_of(i, elem):
        return dofs_ref.at[pl.ds(i * capacity, capacity)][elem]

    unroll = 2

    def block(b, carry):
        first_elem = b * block_elems

        def gather_some(t, c):
            for u in range(unroll):
                g = t * unroll + u
                elem = first_elem + g * groups
                for i in range(nloc):
                    parts = [
                        rows_x[pl.ds(index_of(i, elem + k), 1), :] for k in range(groups)
                    ]
                    gath[pl.ds(i * block_rows + g, 1), :] = pick(parts)
            return c

        lax.fori_loop(0, block_rows // unroll, gather_some, 0)

        scale = scale_ref[pl.ds(pl.multiple_of(b * block_rows, block_rows), block_rows), :]
        values = [gath[i * block_rows : (i + 1) * block_rows, :] for i in range(nloc)]
        for j in range(nloc):
            total = pair_coef[j * nloc] * values[0]
            for i in range(1, nloc):
                total = total + pair_coef[j * nloc + i] * values[i]
            term[j * block_rows : (j + 1) * block_rows, :] = total * scale

        def scatter_some(step):
            def some(t, c):
                for u in range(unroll):
                    g = t * unroll + u
                    elem = first_elem + g * groups
                    for j in range(0, nloc, step):
                        slots = range(j, min(j + step, nloc))
                        new = [term[pl.ds(s * block_rows + g, 1), :] for s in slots]
                        places = [
                            [pl.ds(index_of(s, elem + k), 1) for k in range(groups)]
                            for s in slots
                        ]
                        sums = [
                            [accs[k][at[k], :] + row for k in range(groups)]
                            for at, row in zip(places, new)
                        ]
                        for at, row in zip(places, sums):
                            for k in range(groups):
                                accs[k][at[k], :] = row[k]
                return c

            lax.fori_loop(0, block_rows // unroll, some, 0)

        clash = index_of(nloc, first_elem + block_elems - 1)

        @pl.when(clash == 0)
        def _():
            scatter_some(2)

        @pl.when(clash != 0)
        def _():
            scatter_some(1)

        return carry

    live = count_ref[0]
    lax.fori_loop(0, (live + block_elems - 1) // block_elems, block, 0)

    folder = (iota((2 * width, LANES), 1) % (2 * width) == iota((2 * width, LANES), 0)).astype(BF16)
    folder = jnp.concatenate([folder, folder], axis=1)
    wide = 2 * LANES

    def folded(first):
        at = pl.ds(first, wide)
        total = pick([acc[at, :] for acc in accs])
        return dot_nt(folder, jnp.concatenate(split(total), axis=1))

    def inner(x, y):
        xt, xb = split(x)
        yt, yb = split(y)
        return dot_nt(
            jnp.concatenate([xt, xt, xb], axis=1), jnp.concatenate([yt, yb, yt], axis=1)
        )

    def fold_own(c, gram):
        for u in range(2):
            first = pl.multiple_of(c * 2 * wide + u * wide, wide)
            at = pl.ds(first, wide)
            total = folded(first)
            curl_ref[:, at] = total[:width]
            mass_out_ref[:, at] = total[width:]
            gram = gram + inner(own_ref[:, at], total)
        return gram

    gram = lax.fori_loop(
        0, owned_len // (2 * wide), fold_own, jnp.zeros((width, 2 * width), F32)
    )

    def fold_face(c, gram):
        first = pl.multiple_of(c * wide, wide)
        at = pl.ds(first, wide)
        total = folded(pl.multiple_of(owned_len + first, wide))
        gram = gram + inner(turn_in(high_x_ref[:, at]), total)
        side_x_ref[:width, at] = turn_back(total[:width])
        side_x_ref[width:, at] = turn_back(total[width:])
        total = folded(pl.multiple_of(owned_len + face_len + first, wide))
        gram = gram + inner(high_y_ref[:, at], total)
        side_y_ref[:, at] = total
        return gram

    gram_ref[...] = lax.fori_loop(0, face_len // wide, fold_face, gram)


def all_sum(value, axis):
    count = lax.axis_size(axis)
    step = 1
    total = value
    while step < count:
        total = total + lax.ppermute(total, axis, [(i, i ^ step) for i in range(count)])
        step *= 2
    return total


def on_device(
    trial_block,
    stiff_coef,
    mass_coef,
    elem_count,
    elem_dofs,
    pairing,
    bloch_fraction,
    stiff_ref,
    mass_ref,
):
    own_block = trial_block[0, 0]
    vecs, owned_len = own_block.shape[1:]
    face_len = pairing.shape[0]
    interior = owned_len - 2 * face_len
    width = 2 * vecs
    groups = LANES // (2 * width)
    capacity, nloc = elem_dofs.shape[2:]
    own_rows = own_block.reshape(width, owned_len)
    low_x = own_rows[:, interior : interior + face_len]
    low_y = own_rows[:, interior + face_len :]
    high_x = lax.ppermute(low_x, "px", ring_route("px", -1))
    high_y = lax.ppermute(low_y, "py", line_route("py", -1))
    live = elem_count[0]
    table_rows = -(-(nloc + 1) // 8) * 8
    smem = pl.BlockSpec(memory_space=pltpu.SMEM)
    vmem = pl.BlockSpec(memory_space=pltpu.VMEM)

    table, scale, turn = pl.pallas_call(
        functools.partial(prepare_kernel, owned_len, face_len, width),
        out_shape=(
            jax.ShapeDtypeStruct((table_rows, capacity), jnp.int32),
            jax.ShapeDtypeStruct((capacity // groups, LANES), F32),
            jax.ShapeDtypeStruct((16, LANES), F32),
        ),
        in_specs=[smem] * 2 + [vmem] * 4,
        out_specs=[vmem] * 3,
        name="prepare",
    )(
        live,
        bloch_fraction,
        elem_dofs[0, 0],
        pairing.reshape(-1, LANES),
        stiff_coef[0],
        mass_coef[0],
    )

    extent = owned_len + 2 * face_len
    curl, mass, side_x, side_y, gram = pl.pallas_call(
        functools.partial(element_kernel, width),
        out_shape=(
            jax.ShapeDtypeStruct((width, owned_len), F32),
            jax.ShapeDtypeStruct((width, owned_len), F32),
            jax.ShapeDtypeStruct((2 * width, face_len), F32),
            jax.ShapeDtypeStruct((2 * width, face_len), F32),
            jax.ShapeDtypeStruct((width, 2 * width), F32),
        ),
        in_specs=[smem] * 3 + [pl.BlockSpec(memory_space=pl.ANY)] + [vmem] * 5,
        out_specs=[vmem] * 5,
        scratch_shapes=[
            pltpu.SMEM(((nloc + 1) * capacity,), jnp.int32),
            pltpu.VMEM((nloc * nloc, BLOCK_ROWS, LANES), F32),
            pltpu.VMEM((extent, LANES), F32),
            pltpu.VMEM((nloc * BLOCK_ROWS, LANES), F32),
            pltpu.VMEM((nloc * BLOCK_ROWS, LANES), F32),
            pltpu.SemaphoreType.DMA((nloc + 1,)),
        ]
        + [pltpu.VMEM((extent, LANES), F32)] * groups,
        compiler_params=pltpu.CompilerParams(vmem_limit_bytes=60 * 1024 * 1024),
        name="elements",
    )(live, stiff_ref, mass_ref, table, turn, own_rows, high_x, high_y, scale)

    back_x = lax.ppermute(side_x, "px", ring_route("px", 1))
    back_y = lax.ppermute(side_y, "py", line_route("py", 1))

    def finish(image, part):
        add_x = back_x[part * width : (part + 1) * width]
        add_y = back_y[part * width : (part + 1) * width]
        whole = image.at[:, interior:].add(jnp.concatenate([add_x, add_y], axis=1))
        return whole.reshape(1, 1, 2, vecs, owned_len)

    summed = all_sum(all_sum(gram, "px"), "py")
    parts = summed.reshape(2, vecs, 2, 2, vecs)
    real_part = parts[0, :, :, 0] + parts[1, :, :, 1]
    imag_part = parts[0, :, :, 1] - parts[1, :, :, 0]
    divisor = float(lax.axis_size("px") * lax.axis_size("py") * owned_len)
    gram_out = jnp.stack([real_part, imag_part]).transpose(2, 0, 1, 3) / divisor
    return (finish(curl, 0), finish(mass, 1), gram_out)


def solution(mesh):
    return jax.shard_map(
        on_device,
        mesh=mesh,
        in_specs=(
            P("px", "py", None, None, None),
            P("px", "py", None),
            P("px", "py", None),
            P("px", "py"),
            P("px", "py", None, None),
            P(),
            P(),
            P(),
            P(),
        ),
        out_specs=(P("px", "py", None, None, None), P("px", "py", None, None, None), P()),
        check_vma=False,
    )
```

time: 128 us -> 87.3 us (0.68)
  Pallas kernels: 48.6 us -> 31.9 us
  starting transfers between devices: 44.9 us -> 33.2 us
  local copies, waits for them, and re-layouts: 10.9 us -> 4.42 us
  other arithmetic: 5.91 us -> 0.84 us
  waiting for transfers between devices: 13.8 us -> 15.5 us
  between operations: 2.96 us -> 1.43 us
    pallas_call x2, Pallas kernels: 48.6 us -> 31.9 us  [the longest x1 29.5 us: on_device(): pl.pallas_call(functools.partial(element_kernel, width), out_shape=(jax.S...]
    ppermute x5, starting transfers between devices: 38.3 us -> 26.5 us  [all_sum(): lax.ppermute(total, axis, [(i, i ^ step) for i in range(count)])]
    unnamed x2 -> x0, other arithmetic: 2.69 us -> none
    reshape x2 -> x0, local copies, waits for them, and re-layouts: 2.3 us -> none  [the longest x1 1.54 us: on_device(): flat_dofs = remapped.reshape(-1)]
    another operation x6 -> x0, local copies, waits for them, and re-layouts: 2.02 us -> none  [the longest x2 1.6 us: on_device(): coefs = jnp.stack([stiff_ref.reshape(-1), mass_ref.reshape(-1)], axis=1)]
    ppermute x1, waiting for transfers between devices: 1.49 us -> 3.32 us  [on_device(): back_y = lax.ppermute(side_y, 'py', line_route('py', 1))]
    scatter-add x1, other arithmetic: 1.88 us -> 0.11 us  [finish(): whole = image.at[:, interior:].add(jnp.concatenate([add_x, add_y], axis=1))]
    ppermute x1, waiting for transfers between devices: 0.01 us -> 1.5 us  [on_device(): high_y = lax.ppermute(low_y, 'py', line_route('py', -1))]
  transfers between devices with their start and end apart: 9 -> 9, of which waited for: 6 -> 7; matrix products, arithmetic and copies ran while one was open for 9% -> 2% of each run, Pallas kernels for 1% -> 3%
where the time goes in v1:
time: 87.3 us
  starting transfers between devices  33.2 us (38%)
  Pallas kernels  31.9 us (37%)
  waiting for transfers between devices  15.5 us (18%)
  local copies, waits for them, and re-layouts  4.42 us (5%)
  between operations  1.43 us (2%)
    pallas_call x1, Pallas kernels, on_device(): pl.pallas_call(functools.partial(element_kernel, width), out_shape=(jax.S...  29.5 us
    ppermute x5, starting transfers between devices, all_sum(): lax.ppermute(total, axis, [(i, i ^ step) for i in range(count)])  26.5 us
    ppermute x5, waiting for transfers between devices, all_sum(): lax.ppermute(total, axis, [(i, i ^ step) for i in range(count)])  7.94 us
    ppermute x1, starting transfers between devices, on_device(): high_x = lax.ppermute(low_x, 'px', ring_route('px', -1))  3.41 us
    ppermute x1, waiting for transfers between devices, on_device(): back_y = lax.ppermute(side_y, 'py', line_route('py', 1))  3.32 us
    unnamed x16, local copies, waits for them, and re-layouts  3.25 us
    ppermute x1, waiting for transfers between devices, on_device(): back_x = lax.ppermute(side_x, 'px', ring_route('px', 1))  2.76 us
    pallas_call x1, Pallas kernels, on_device(): pl.pallas_call(functools.partial(prepare_kernel, owned_len, face_len, wid...  2.37 us
  transfers between devices with their start and end apart: 9, of which 7 were waited for; matrix products, arithmetic and copies ran while one was open for 2% of the time, Pallas kernels for 3%

profile of v1, /device:TPU:0, one launch (start us, length us, event | category | flops | bytes accessed | tf_op | source)
XLA Modules:
  0.0 87.3 jit_solution(4206295649115770766)
XLA Ops:
  0.6 0.0 copy-start.6
  0.6 1.0 %fusion.5 = (f32[16,2048]{1,0:T(8,128)S(1)}, f32[16,2048]{1,0:T(8,128)S(1)}) fusion(f32[16,8192]{1,0:T(8,128)} %bitcast.17), kind=kLoop, calls=%fused_computation.10 | loop fusion | bytes 524288 | tf_op jit(solution)/shard_map/slice | solution.py:364
  1.7 3.4 %collective-permute-start = (f32[16,2048]{1,0:T(8,128)S(1)}, f32[16,2048]{1,0:T(8,128)S(1)}, u32[]{:S(2)}, u32[]{:S(2)}) collective-permute-start(f32[16,2048]{1,0:T(8,128)S(1)} %get-tuple-element.47), channel_id=1, source_target_pairs={{0,28},{4,0},{8,4},{12,8},{16,12},{20,16},{24,20},{28,24},{1,29},{... | collective-permute-start | bytes 393224 | tf_op jit(solution)/shard_map/ppermute | solution.py:365
  5.1 1.3 %collective-permute-start.1 = (f32[16,2048]{1,0:T(8,128)S(1)}, f32[16,2048]{1,0:T(8,128)S(1)}, u32[]{:S(2)}, u32[]{:S(2)}) collective-permute-start(f32[16,2048]{1,0:T(8,128)S(1)} %get-tuple-element.46), channel_id=1, source_target_pairs={{1,0},{2,1},{3,2},{5,4},{6,5},{7,6},{9,8},{10,9},{11,10},{13,12},{... | collective-permute-start | bytes 393224 | tf_op jit(solution)/shard_map/ppermute | solution.py:366
  7.0 0.0 copy-done.6
  7.0 1.0 %copy.12 = s32[1,1,1024,20]{3,2,1,0:T(8,128)} copy(s32[1,1,1024,20]{2,1,3,0:T(1,128)S(1)} %copy-done.6) | data formatting | bytes 163840 | tf_op args[4]
  8.0 2.4 %prepare.1 = (s32[24,1024]{1,0:T(8,128)}, f32[256,128]{1,0:T(8,128)}, f32[16,128]{1,0:T(8,128)}) custom-call(s32[1]{0:T(128)} %bitcast.14.count_ref, s32[2]{0:T(128)} %bloch_ref.1, s32[1024,20]{1,0:T(8,128)} %bitcast.16, s32[16,128]{1,0:T(8,128)} %bitcast.21, f32[1,1024]{1,0:T(1,128)} %bitcast.22, f32[1,1024]{1,0:T(1,128)} %bitcast.23), custom_call_target="tpu_custom_call" | custom-call | tf_op jit(solution)/shard_map/prepare/pallas_call | solution.py:372
  10.4 0.0 collective-permute-done.high_x_ref
  10.4 0.0 copy-start.4
  10.4 1.5 %collective-permute-done.1.high_y_ref = f32[16,2048]{1,0:T(8,128)S(1)} collective-permute-done((f32[16,2048]{1,0:T(8,128)S(1)}, f32[16,2048]{1,0:T(8,128)S(1)}, u32[]{:S(2)}, u32[]{:S(2)}) %collective-permute-start.1) | collective-permute-done | bytes 131104 | tf_op jit(solution)/shard_map/ppermute | solution.py:366
  11.9 0.0 copy-start.5
  11.9 0.0 copy-done.4
  11.9 0.6 copy-done.5
  12.6 29.5 %elements.1 = (f32[16,8192]{1,0:T(8,128)}, f32[16,8192]{1,0:T(8,128)}, f32[32,2048]{1,0:T(8,128)}, f32[32,2048]{1,0:T(8,128)}, f32[16,32]{1,0:T(8,128)}) custom-call(s32[1]{0:T(128)} %bitcast.15.count_ref, f32[20,20]{1,0:T(8,128)} %stiff_ref.1, f32[20,20]{1,0:T(8,128)} %mass_ref.1, s32[24,1024]{1,0:T(8,128)} %get-tuple-element.35.table_hbm, ...), custom_call_target="tpu_custom_call" | custom-call | tf_op jit(solution)/shard_map/elements/pallas_call | solution.py:392
  42.1 0.5 collective-permute-start.4
  42.6 1.0 %collective-permute-done.4 = f32[16,32]{1,0:T(8,128)S(1)} collective-permute-done((f32[16,32]{1,0:T(8,128)}, f32[16,32]{1,0:T(8,128)S(1)}, u32[]{:S(2)}, u32[]{:S(2)}) %collective-permute-start.4) | collective-permute-done | bytes 2080 | tf_op jit(solution)/shard_map/ppermute | solution.py:339
  43.7 0.7 add.44
  44.4 4.8 %collective-permute-start.5 = (f32[16,32]{1,0:T(8,128)S(1)}, f32[16,32]{1,0:T(8,128)S(1)}, u32[]{:S(2)}, u32[]{:S(2)}) collective-permute-start(f32[16,32]{1,0:T(8,128)S(1)} %add.44), channel_id=1, source_target_pairs={{0,8},{4,12},{8,0},{12,4},{16,24},{20,28},{24,16},{28,20},{1,9},{5... | collective-permute-start | bytes 6152 | tf_op jit(solution)/shard_map/ppermute | solution.py:339
  49.2 1.6 %collective-permute-done.5 = f32[16,32]{1,0:T(8,128)S(1)} collective-permute-done((f32[16,32]{1,0:T(8,128)S(1)}, f32[16,32]{1,0:T(8,128)S(1)}, u32[]{:S(2)}, u32[]{:S(2)}) %collective-permute-start.5) | collective-permute-done | bytes 2080 | tf_op jit(solution)/shard_map/ppermute | solution.py:339
  50.9 0.0 collective-permute-start.6
  50.9 3.6 %collective-permute-done.6 = f32[16,32]{1,0:T(8,128)S(1)} collective-permute-done((f32[16,32]{1,0:T(8,128)S(1)}, f32[16,32]{1,0:T(8,128)S(1)}, u32[]{:S(2)}, u32[]{:S(2)}) %collective-permute-start.6) | collective-permute-done | bytes 2080 | tf_op jit(solution)/shard_map/ppermute | solution.py:339
  54.5 18.1 %collective-permute-start.7 = (f32[16,32]{1,0:T(8,128)S(1)}, f32[16,32]{1,0:T(8,128)S(1)}, u32[]{:S(2)}, u32[]{:S(2)}) collective-permute-start(f32[16,32]{1,0:T(8,128)S(1)} %add.46), channel_id=1, source_target_pairs={{0,1},{1,0},{2,3},{3,2},{4,5},{5,4},{6,7},{7,6},{8,9},{9,8},{10,11... | collective-permute-start | bytes 6152 | tf_op jit(solution)/shard_map/ppermute | solution.py:339
  72.6 1.6 %collective-permute-done.7 = f32[16,32]{1,0:T(8,128)S(1)} collective-permute-done((f32[16,32]{1,0:T(8,128)S(1)}, f32[16,32]{1,0:T(8,128)S(1)}, u32[]{:S(2)}, u32[]{:S(2)}) %collective-permute-start.7) | collective-permute-done | bytes 2080 | tf_op jit(solution)/shard_map/ppermute | solution.py:339
  74.2 3.0 %collective-permute-start.8 = (f32[16,32]{1,0:T(8,128)S(1)}, f32[16,32]{1,0:T(8,128)S(1)}, u32[]{:S(2)}, u32[]{:S(2)}) collective-permute-start(f32[16,32]{1,0:T(8,128)S(1)} %add.47), channel_id=1, source_target_pairs={{0,2},{1,3},{2,0},{3,1},{4,6},{5,7},{6,4},{7,5},{8,10},{9,11},{10,... | collective-permute-start | bytes 6152 | tf_op jit(solution)/shard_map/ppermute | solution.py:339
  77.3 1.9 %collective-permute-start.3 = (f32[32,2048]{1,0:T(8,128)}, f32[32,2048]{1,0:T(8,128)S(1)}, u32[]{:S(2)}, u32[]{:S(2)}) collective-permute-start(f32[32,2048]{1,0:T(8,128)} %get-tuple-element.40), channel_id=1, source_target_pairs={{0,1},{1,2},{2,3},{4,5},{5,6},{6,7},{8,9},{9,10},{10,11},{12,13},{... | collective-permute-start | bytes 786440 | tf_op jit(solution)/shard_map/ppermute | solution.py:417
  79.2 0.1 collective-permute-start.2
  79.3 0.0 collective-permute-done.8
  79.3 0.1 reshape.106
  79.4 0.6 copy.17
  80.1 0.0 copy-start
  80.1 0.0 copy-start.2
  80.1 3.3 %collective-permute-done.3 = f32[32,2048]{1,0:T(8,128)S(1)} collective-permute-done((f32[32,2048]{1,0:T(8,128)}, f32[32,2048]{1,0:T(8,128)S(1)}, u32[]{:S(2)}, u32[]{:S(2)}) %collective-permute-start.3) | collective-permute-done | bytes 262176 | tf_op jit(solution)/shard_map/ppermute | solution.py:417
  83.4 2.8 %collective-permute-done.2 = f32[32,2048]{1,0:T(8,128)S(1)} collective-permute-done((f32[32,2048]{1,0:T(8,128)}, f32[32,2048]{1,0:T(8,128)S(1)}, u32[]{:S(2)}, u32[]{:S(2)}) %collective-permute-start.2) | collective-permute-done | bytes 262176 | tf_op jit(solution)/shard_map/ppermute | solution.py:416
  86.2 0.0 copy-done
  86.2 0.0 copy-done.2
  86.2 0.1 fusion
  86.3 0.0 copy-start.1
  86.3 0.0 copy-start.3
  86.3 0.8 copy-done.1
  87.1 0.2 copy-done.3
  (9 shorter events, 0.1 us)
Async XLA Ops:
  0.6 6.4 %copy-start.6 = (s32[1,1,1024,20]{2,1,3,0:T(1,128)S(1)}, s32[1,1,1024,20]{2,1,3,0:T(1,128)}, u32[]{:S(2)}) copy-start(s32[1,1,1024,20]{2,1,3,0:T(1,128)} %param.17) | copy-start | bytes 245764
  1.7 8.8 %collective-permute-start = (f32[16,2048]{1,0:T(8,128)S(1)}, f32[16,2048]{1,0:T(8,128)S(1)}, u32[]{:S(2)}, u32[]{:S(2)}) collective-permute-start(f32[16,2048]{1,0:T(8,128)S(1)} %get-tuple-element.47), channel_id=1, source_target_pairs={{0,28},{4,0},{8,4},{12,8},{16,12},{20,16},{24,20},{28,24},{1,29},{... | collective-permute-start | bytes 393224 | tf_op jit(solution)/shard_map/ppermute | solution.py:365
  5.1 6.8 %collective-permute-start.1 = (f32[16,2048]{1,0:T(8,128)S(1)}, f32[16,2048]{1,0:T(8,128)S(1)}, u32[]{:S(2)}, u32[]{:S(2)}) collective-permute-start(f32[16,2048]{1,0:T(8,128)S(1)} %get-tuple-element.46), channel_id=1, source_target_pairs={{1,0},{2,1},{3,2},{5,4},{6,5},{7,6},{9,8},{10,9},{11,10},{13,12},{... | collective-permute-start | bytes 393224 | tf_op jit(solution)/shard_map/ppermute | solution.py:366
  10.4 1.5 %copy-start.4 = (f32[16,2048]{1,0:T(8,128)}, f32[16,2048]{1,0:T(8,128)S(1)}, u32[]{:S(2)}) copy-start(f32[16,2048]{1,0:T(8,128)S(1)} %collective-permute-done.high_x_ref) | copy-start | bytes 393220
  11.9 0.7 copy-start.5
  42.1 1.6 %collective-permute-start.4 = (f32[16,32]{1,0:T(8,128)}, f32[16,32]{1,0:T(8,128)S(1)}, u32[]{:S(2)}, u32[]{:S(2)}) collective-permute-start(f32[16,32]{1,0:T(8,128)} %get-tuple-element.42), channel_id=1, source_target_pairs={{0,4},{4,0},{8,12},{12,8},{16,20},{20,16},{24,28},{28,24},{1,5},{5... | collective-permute-start | bytes 6152 | tf_op jit(solution)/shard_map/ppermute | solution.py:339
  44.4 6.5 %collective-permute-start.5 = (f32[16,32]{1,0:T(8,128)S(1)}, f32[16,32]{1,0:T(8,128)S(1)}, u32[]{:S(2)}, u32[]{:S(2)}) collective-permute-start(f32[16,32]{1,0:T(8,128)S(1)} %add.44), channel_id=1, source_target_pairs={{0,8},{4,12},{8,0},{12,4},{16,24},{20,28},{24,16},{28,20},{1,9},{5... | collective-permute-start | bytes 6152 | tf_op jit(solution)/shard_map/ppermute | solution.py:339
  50.9 3.7 %collective-permute-start.6 = (f32[16,32]{1,0:T(8,128)S(1)}, f32[16,32]{1,0:T(8,128)S(1)}, u32[]{:S(2)}, u32[]{:S(2)}) collective-permute-start(f32[16,32]{1,0:T(8,128)S(1)} %add.45), channel_id=1, source_target_pairs={{0,16},{4,20},{8,24},{12,28},{16,0},{20,4},{24,8},{28,12},{1,17},{... | collective-permute-start | bytes 6152 | tf_op jit(solution)/shard_map/ppermute | solution.py:339
  54.5 19.7 %collective-permute-start.7 = (f32[16,32]{1,0:T(8,128)S(1)}, f32[16,32]{1,0:T(8,128)S(1)}, u32[]{:S(2)}, u32[]{:S(2)}) collective-permute-start(f32[16,32]{1,0:T(8,128)S(1)} %add.46), channel_id=1, source_target_pairs={{0,1},{1,0},{2,3},{3,2},{4,5},{5,4},{6,7},{7,6},{8,9},{9,8},{10,11... | collective-permute-start | bytes 6152 | tf_op jit(solution)/shard_map/ppermute | solution.py:339
  74.2 5.0 %collective-permute-start.8 = (f32[16,32]{1,0:T(8,128)S(1)}, f32[16,32]{1,0:T(8,128)S(1)}, u32[]{:S(2)}, u32[]{:S(2)}) collective-permute-start(f32[16,32]{1,0:T(8,128)S(1)} %add.47), channel_id=1, source_target_pairs={{0,2},{1,3},{2,0},{3,1},{4,6},{5,7},{6,4},{7,5},{8,10},{9,11},{10,... | collective-permute-start | bytes 6152 | tf_op jit(solution)/shard_map/ppermute | solution.py:339
  77.3 6.1 %collective-permute-start.3 = (f32[32,2048]{1,0:T(8,128)}, f32[32,2048]{1,0:T(8,128)S(1)}, u32[]{:S(2)}, u32[]{:S(2)}) collective-permute-start(f32[32,2048]{1,0:T(8,128)} %get-tuple-element.40), channel_id=1, source_target_pairs={{0,1},{1,2},{2,3},{4,5},{5,6},{6,7},{8,9},{9,10},{10,11},{12,13},{... | collective-permute-start | bytes 786440 | tf_op jit(solution)/shard_map/ppermute | solution.py:417
  79.2 7.0 %collective-permute-start.2 = (f32[32,2048]{1,0:T(8,128)}, f32[32,2048]{1,0:T(8,128)S(1)}, u32[]{:S(2)}, u32[]{:S(2)}) collective-permute-start(f32[32,2048]{1,0:T(8,128)} %get-tuple-element.39), channel_id=1, source_target_pairs={{0,4},{4,8},{8,12},{12,16},{16,20},{20,24},{24,28},{28,0},{1,5},{5... | collective-permute-start | bytes 786440 | tf_op jit(solution)/shard_map/ppermute | solution.py:416
  80.1 6.1 %copy-start = (f32[16,8192]{1,0:T(8,128)S(1)}, f32[16,8192]{1,0:T(8,128)}, u32[]{:S(2)}) copy-start(f32[16,8192]{1,0:T(8,128)} %get-tuple-element.38) | copy-start | bytes 1572868
  80.1 6.1 %copy-start.2 = (f32[16,8192]{1,0:T(8,128)S(1)}, f32[16,8192]{1,0:T(8,128)}, u32[]{:S(2)}) copy-start(f32[16,8192]{1,0:T(8,128)} %get-tuple-element.41) | copy-start | bytes 1572868
  86.3 0.8 copy-start.1
  86.3 1.0 %copy-start.3 = (f32[16,8192]{1,0:T(8,128)}, f32[16,8192]{1,0:T(8,128)S(1)}, u32[]{:S(2)}) copy-start(f32[16,8192]{1,0:T(8,128)S(1)} %get-tuple-element.57) | copy-start | bytes 1572868
